TPU v7x, 256 devices: a whole 4x4x8 slice. The times are simulated.
256 devices in a mesh: dp: 8 (over x, z_hi), context: 32 (over y, z_lo, core).
Axes of the slice: x: 4, y: 4, z: 8 (z_hi: 2, z_lo: 4; z = z_hi * 4 + z_lo), core: 2. Of those that a mesh axis runs over, the one named last changes fastest.
Arguments:
- grad_out: bfloat16 [8, 4096, 4096], P('dp', 'context'), may hold values from -6 to 6
- attn: bfloat16 [8, 4096, 4096], P('dp', 'context'), may hold values from -0.032958984 to 0.032958984
- w_out: bfloat16 [4096, 4096], P('context'), may hold values from -0.09375 to 0.09375
Outputs:
- grad_attn: bfloat16 [8, 4096, 4096], P('dp', None, 'context')
- grad_w: bfloat16 [4096, 4096], P('context')
All inputs are finite; a program needn't handle non-finite values.
Results may differ from a plain program's by a relative error of at most 0.013.
Values may be sent and summed in bfloat16 or wider, within the bound.
No kernel may reach another device: no remote copies, remote signals or barrier semaphores. Data moves between devices by JAX's collectives and lax.ppermute only.
A program may use at most 128 MiB of HBM per device.

v0:
```python
import jax
import jax.numpy as jnp
from jax import lax
from jax.sharding import Mesh, PartitionSpec as P

CHUNKS = (2048, 2048)
RING8 = ("h", "l")


def shift(v, axis, by):
    n = lax.axis_size(axis)
    return lax.ppermute(v, axis, [(i, (i + by) % n) for i in range(n)])


def exchange(v, axis):
    return lax.all_to_all(v, axis, split_axis=0, concat_axis=0, tiled=True)


def after(v, *others):
    return lax.optimization_barrier((v, *others))[0]


def around(own, axis):
    half = own.shape[0] // 2
    above = shift(own, axis, -1)
    below = shift(own, axis, 1)
    far_a = shift(above[:half], axis, -1)
    far_b = shift(below[half:], axis, 1)
    return [own, above, far_a, far_b, below]


def local(grad_out, attn, w_out):
    f32, bf16 = (jnp.float32, jnp.bfloat16)
    g = grad_out[0]
    a = attn[0]
    toks, feats = g.shape
    heads = w_out.shape[0]
    quarter = heads // 4
    l = lax.axis_index("l")
    cuts, at = ([], 0)
    for size in CHUNKS:
        size = size * feats // sum(CHUNKS)
        cuts.append((at, at + size))
        at += size
    g_cols = [lax.all_gather(g[:, lo:hi], ("y", "c"), axis=0, tiled=True) for lo, hi in cuts]
    a = a.reshape(toks, 4, 4, 2, heads).transpose(1, 3, 0, 2, 4).reshape(8, toks, 4 * heads)
    acts = exchange(a, ("y", "c")).reshape(8 * toks, 4 * heads)
    w_parts = around(w_out, RING8)
    sums, part = ([], None)
    for gj in g_cols:
        if part is not None:
            gj = after(gj, part)
        part = lax.dot_general(
            acts, gj, (((0,), (0,)), ((), ())), preferred_element_type=f32
        ).astype(bf16)
        part = part.reshape(4, 4, quarter, -1)
        tot = exchange(part.transpose(1, 0, 2, 3), "x").astype(f32).sum(0).astype(bf16)
        tot = exchange(tot, "l").astype(f32).sum(0).astype(bf16)
        tot = (tot.astype(f32) + shift(tot, "h", 1).astype(f32)).astype(bf16)
        sums.append(exchange(jnp.broadcast_to(tot[None], (4,) + tot.shape), "x").reshape(heads, -1))
    grad_w = jnp.concatenate(sums, 1)
    w = jnp.concatenate(w_parts, 0)
    w = lax.dynamic_slice_in_dim(jnp.concatenate([w, w], 0), (4 - l & 3) * heads, 4 * heads, 0)
    gall = after(jnp.concatenate(g_cols, 1), part)
    res = lax.dot_general(gall, w, (((1,), (1,)), ((), ())), preferred_element_type=f32).astype(
        bf16
    )
    res = res.reshape(8 * toks, 4, heads).transpose(1, 0, 2)
    out = exchange(res, "l")
    out = out.reshape(4, 4, 2 * toks, heads).transpose(1, 0, 2, 3).reshape(1, 4 * 8 * toks, heads)
    return (out, grad_w)


def solution(mesh):
    fine = Mesh(mesh.devices.reshape(4, 2, 4, 4, 2), ("x", "h", "y", "l", "c"))
    dp, context = (("x", "h"), ("y", "l", "c"))
    in_specs = (P(dp, context, None), P(dp, context, None), P(context, None))
    out_specs = (P(dp, None, context), P(context, None))
    return jax.shard_map(local, mesh=fine, in_specs=in_specs, out_specs=out_specs, check_vma=False)
```

profile of v0, /device:TPU:2, one launch (start us, length us, event | category | flops | bytes accessed | tf_op | source)
XLA Modules:
  0.0 265.9 jit_solution(8318306603552850730)
XLA Ops:
  10.4 5.9 %collective-permute-start = (bf16[128,4096]{1,0:T(8,128)(2,1)}, bf16[128,4096]{1,0:T(8,128)(2,1)S(1)}, u32[]{:S(2)}, u32[]{:S(2)}) collective-permute-start(bf16[128,4096]{1,0:T(8,128)(2,1)} %param.5), channel_id=1, source_target_pairs={{0,38},{2,0},{4,2},{6,4},{32,6},{34,32},{36,34},{38,36},{1,39},{3,... | collective-permute-start | bytes 3145736 | tf_op jit(solution)/shard_map/ppermute | solution.py:12
  20.9 4.5 %all-to-all-start = ((bf16[8,128,512]{1,2,0:T(8,128)(2,1)}), bf16[8,128,512]{1,2,0:T(8,128)(2,1)}, u32[]{:S(2)}, u32[]{:S(2)}) async-start(bf16[8,128,512]{1,2,0:T(8,128)(2,1)} %bitcast.33), calls=%async_computation | async-start | bytes 2097152 | tf_op jit(solution)/shard_map/all_to_all | solution.py:16
  26.4 26.3 %all-to-all-done = bf16[8,128,512]{1,2,0:T(8,128)(2,1)} async-done(((bf16[8,128,512]{1,2,0:T(8,128)(2,1)}), bf16[8,128,512]{1,2,0:T(8,128)(2,1)}, u32[]{:S(2)}, u32[]{:S(2)}) %all-to-all-start) | async-done | bytes 1048608 | tf_op jit(solution)/shard_map/all_to_all | solution.py:16
  55.1 3.2 %collective-permute-start.1 = (bf16[64,4096]{1,0:T(8,128)(2,1)}, bf16[64,4096]{1,0:T(8,128)(2,1)}, u32[]{:S(2)}, u32[]{:S(2)}) collective-permute-start(bf16[64,4096]{1,0:T(8,128)(2,1)} %slice.18), channel_id=1, source_target_pairs={{0,38},{2,0},{4,2},{6,4},{32,6},{34,32},{36,34},{38,36},{1,39},{3,... | collective-permute-start | bytes 1572872 | tf_op jit(solution)/shard_map/ppermute | solution.py:12
  59.1 5.9 %convolution_convert_fusion.1 = bf16[512,2048]{1,0:T(8,128)(2,1)} fusion(bf16[1024,512]{1,0:T(8,128)(2,1)S(1)} %bitcast.40, bf16[1024,2048]{1,0:T(8,128)(2,1)} %all-gather.3.cloned.1.call-done), kind=kOutput, calls=%fused_computation.4 | convolution fusion | flops 2148532224 | bytes 7340032 | tf_op jit(solution)/shard_map/dot_general | solution.py:53
  65.0 28.4 %all-gather.5.cloned.1.call-done = bf16[1024,2048]{1,0:T(8,128)(2,1)} async-done(((bf16[128,2048]{1,0:T(8,128)(2,1)}), bf16[1024,2048]{1,0:T(8,128)(2,1)}) %all-gather.5.cloned.1.call-update) | async-done | bytes 4194320 | tf_op jit(solution)/shard_map/all_gather | solution.py:45
  93.4 4.6 %convolution_convert_fusion = bf16[2048,512]{0,1:T(8,128)(2,1)S(1)} fusion(bf16[1024,2048]{1,0:T(8,128)(2,1)} %all-gather.5.cloned.1.call-done, bf16[1024,512]{1,0:T(8,128)(2,1)S(1)} %bitcast.41), kind=kOutput, calls=%fused_computation.3 | convolution fusion | flops 2148532224 | bytes 7340032 | tf_op jit(solution)/shard_map/dot_general | solution.py:53
  99.6 4.8 %all-to-all-start.5 = ((bf16[4,4,32,2048]{3,2,1,0:T(8,128)(2,1)}), bf16[4,4,32,2048]{3,2,1,0:T(8,128)(2,1)S(1)}, u32[]{:S(2)}, u32[]{:S(2)}) async-start(bf16[4,4,32,2048]{3,2,1,0:T(8,128)(2,1)} %bitcast.31), calls=%async_computation.5 | async-start | bytes 4194304 | tf_op jit(solution)/shard_map/all_to_all | solution.py:16
  111.5 3.2 %copy.26 = bf16[4,4,32,2048]{3,2,0,1:T(8,128)(2,1)} copy(bf16[4,4,32,2048]{3,2,1,0:T(8,128)(2,1)} %bitcast.35) | data formatting | bytes 4194304 | tf_op jit(solution)/shard_map/reshape | solution.py:56
  114.8 14.9 %all-to-all-done.5 = bf16[4,4,32,2048]{3,2,1,0:T(8,128)(2,1)S(1)} async-done(((bf16[4,4,32,2048]{3,2,1,0:T(8,128)(2,1)}), bf16[4,4,32,2048]{3,2,1,0:T(8,128)(2,1)S(1)}, u32[]{:S(2)}, u32[]{:S(2)}) %all-to-all-start.5) | async-done | bytes 2097184 | tf_op jit(solution)/shard_map/all_to_all | solution.py:16
  129.7 5.9 %all-to-all-start.2 = ((bf16[4,4,32,2048]{3,2,1,0:T(8,128)(2,1)}), bf16[4,4,32,2048]{3,2,1,0:T(8,128)(2,1)}, u32[]{:S(2)}, u32[]{:S(2)}) async-start(bf16[4,4,32,2048]{3,2,1,0:T(8,128)(2,1)} %bitcast.32), calls=%async_computation.2 | async-start | bytes 4194304 | tf_op jit(solution)/shard_map/all_to_all | solution.py:16
  145.3 14.9 %all-to-all-done.2 = bf16[4,4,32,2048]{3,2,1,0:T(8,128)(2,1)} async-done(((bf16[4,4,32,2048]{3,2,1,0:T(8,128)(2,1)}), bf16[4,4,32,2048]{3,2,1,0:T(8,128)(2,1)}, u32[]{:S(2)}, u32[]{:S(2)}) %all-to-all-start.2) | async-done | bytes 2097184 | tf_op jit(solution)/shard_map/all_to_all | solution.py:16
  160.1 4.8 %all-to-all-start.6 = ((bf16[4,32,2048]{2,1,0:T(8,128)(2,1)}), bf16[4,32,2048]{2,1,0:T(8,128)(2,1)S(1)}, u32[]{:S(2)}, u32[]{:S(2)}) async-start(bf16[4,32,2048]{2,1,0:T(8,128)(2,1)} %reduce_sum.50), calls=%async_computation.6 | async-start | bytes 1048576 | tf_op jit(solution)/shard_map/all_to_all | solution.py:16
  166.1 7.8 %pad_maximum_fusion = bf16[1024,4096]{1,0:T(8,128)(2,1)} fusion(bf16[1024,2048]{1,0:T(8,128)(2,1)} %all-gather.5.cloned.1.call-done, bf16[1024,2048]{1,0:T(8,128)(2,1)} %all-gather.3.cloned.1.call-done), kind=kLoop, calls=%fused_computation | loop fusion | flops 16777216 | bytes 16777216 | tf_op jit(solution)/shard_map/concatenate | solution.py:64
  177.8 4.1 %all-to-all-start.3 = ((bf16[4,32,2048]{2,1,0:T(8,128)(2,1)}), bf16[4,32,2048]{2,1,0:T(8,128)(2,1)S(1)}, u32[]{:S(2)}, u32[]{:S(2)}) async-start(bf16[4,32,2048]{2,1,0:T(8,128)(2,1)} %reduce_sum.48), calls=%async_computation.3 | async-start | bytes 1048576 | tf_op jit(solution)/shard_map/all_to_all | solution.py:16
  181.9 10.1 %fusion.2 = bf16[1024,512]{0,1:T(8,128)(2,1)} fusion(bf16[1024,4096]{1,0:T(8,128)(2,1)} %pad_maximum_fusion, bf16[1024,4096]{1,0:T(8,128)(2,1)} %constant_dynamic-update-slice_fusion, s32[]{:T(128)S(6)} %select_n.3), kind=kOutput, calls=%fused_computation.7 | convolution fusion | flops 4295491584 | bytes 13631492 | tf_op jit(solution)/shard_map/dot_general | solution.py:65
  194.2 3.5 %all-to-all-start.1 = ((bf16[4,1024,128]{1,2,0:T(8,128)(2,1)}), bf16[4,1024,128]{1,2,0:T(8,128)(2,1)S(1)}, u32[]{:S(2)}, u32[]{:S(2)}) async-start(bf16[4,1024,128]{1,2,0:T(8,128)(2,1)} %bitcast.9), calls=%async_computation.1 | async-start | bytes 2097152 | tf_op jit(solution)/shard_map/all_to_all | solution.py:16
  197.8 5.1 %collective-permute-start.5 = (bf16[32,2048]{1,0:T(8,128)(2,1)S(1)}, bf16[32,2048]{1,0:T(8,128)(2,1)S(1)}, u32[]{:S(2)}, u32[]{:S(2)}) collective-permute-start(bf16[32,2048]{1,0:T(8,128)(2,1)S(1)} %reduce_sum.51), channel_id=1, source_target_pairs={{0,32},{32,0},{1,33},{33,1},{2,34},{34,2},{3,35},{35,3},{4,36},{36... | collective-permute-start | bytes 393224 | tf_op jit(solution)/shard_map/ppermute | solution.py:12
  204.0 24.7 %collective-permute-done.5 = bf16[32,2048]{1,0:T(8,128)(2,1)S(1)} collective-permute-done((bf16[32,2048]{1,0:T(8,128)(2,1)S(1)}, bf16[32,2048]{1,0:T(8,128)(2,1)S(1)}, u32[]{:S(2)}, u32[]{:S(2)}) %collective-permute-start.5) | collective-permute-done | bytes 131104 | tf_op jit(solution)/shard_map/ppermute | solution.py:12
  228.7 3.7 %all-to-all-done.1 = bf16[4,1024,128]{1,2,0:T(8,128)(2,1)S(1)} async-done(((bf16[4,1024,128]{1,2,0:T(8,128)(2,1)}), bf16[4,1024,128]{1,2,0:T(8,128)(2,1)S(1)}, u32[]{:S(2)}, u32[]{:S(2)}) %all-to-all-start.1) | async-done | bytes 1048608 | tf_op jit(solution)/shard_map/all_to_all | solution.py:16
  233.2 4.9 %all-to-all-start.7 = ((bf16[4,32,2048]{2,1,0:T(8,128)(2,1)}), bf16[4,32,2048]{2,1,0:T(8,128)(2,1)S(1)}, u32[]{:S(2)}, u32[]{:S(2)}) async-start(bf16[4,32,2048]{2,1,0:T(8,128)(2,1)} %broadcast_in_dim.5), calls=%async_computation.7 | async-start | bytes 1048576 | tf_op jit(solution)/shard_map/all_to_all | solution.py:16
  238.2 7.5 %all-to-all-done.7 = bf16[4,32,2048]{2,1,0:T(8,128)(2,1)S(1)} async-done(((bf16[4,32,2048]{2,1,0:T(8,128)(2,1)}), bf16[4,32,2048]{2,1,0:T(8,128)(2,1)S(1)}, u32[]{:S(2)}, u32[]{:S(2)}) %all-to-all-start.7) | async-done | bytes 524320 | tf_op jit(solution)/shard_map/all_to_all | solution.py:16
  246.5 4.9 %all-to-all-start.4 = ((bf16[4,32,2048]{2,1,0:T(8,128)(2,1)}), bf16[4,32,2048]{2,1,0:T(8,128)(2,1)S(1)}, u32[]{:S(2)}, u32[]{:S(2)}) async-start(bf16[4,32,2048]{2,1,0:T(8,128)(2,1)} %broadcast_in_dim.4), calls=%async_computation.4 | async-start | bytes 1048576 | tf_op jit(solution)/shard_map/all_to_all | solution.py:16
  253.6 4.4 %all-to-all-done.4 = bf16[4,32,2048]{2,1,0:T(8,128)(2,1)S(1)} async-done(((bf16[4,32,2048]{2,1,0:T(8,128)(2,1)}), bf16[4,32,2048]{2,1,0:T(8,128)(2,1)S(1)}, u32[]{:S(2)}, u32[]{:S(2)}) %all-to-all-start.4) | async-done | bytes 524320 | tf_op jit(solution)/shard_map/all_to_all | solution.py:16
  (47 shorter events, 43.9 us)
Async XLA Ops:
  7.2 18.2 %copy-start.1 = (bf16[128,4096]{1,0:T(8,128)(2,1)S(1)}, bf16[128,4096]{1,0:T(8,128)(2,1)}, u32[]{:S(2)}) copy-start(bf16[128,4096]{1,0:T(8,128)(2,1)} %param.5) | copy-start | bytes 3145732
  7.2 51.9 %all-gather.3.cloned.1.call-start = ((), (), s32[]{:S(2)}) async-start(), calls=%async_computation.8 | async-start | bytes 4718592 | tf_op jit(solution)/shard_map/all_gather | solution.py:45
  9.6 83.8 %all-gather.5.cloned.1.call-start = ((), (), s32[]{:S(2)}) async-start(), calls=%async_computation.9 | async-start | bytes 4718592 | tf_op jit(solution)/shard_map/all_gather | solution.py:45
  10.4 43.8 %collective-permute-start = (bf16[128,4096]{1,0:T(8,128)(2,1)}, bf16[128,4096]{1,0:T(8,128)(2,1)S(1)}, u32[]{:S(2)}, u32[]{:S(2)}) collective-permute-start(bf16[128,4096]{1,0:T(8,128)(2,1)} %param.5), channel_id=1, source_target_pairs={{0,38},{2,0},{4,2},{6,4},{32,6},{34,32},{36,34},{38,36},{1,39},{3,... | collective-permute-start | bytes 3145736 | tf_op jit(solution)/shard_map/ppermute | solution.py:12
  16.3 42.0 %collective-permute-start.2 = (bf16[128,4096]{1,0:T(8,128)(2,1)}, bf16[128,4096]{1,0:T(8,128)(2,1)S(1)}, u32[]{:S(2)}, u32[]{:S(2)}) collective-permute-start(bf16[128,4096]{1,0:T(8,128)(2,1)} %param.5), channel_id=1, source_target_pairs={{0,2},{2,4},{4,6},{6,32},{32,34},{34,36},{36,38},{38,0},{1,3},{3,5... | collective-permute-start | bytes 3145736 | tf_op jit(solution)/shard_map/ppermute | solution.py:12
  20.9 31.8 %all-to-all-start = ((bf16[8,128,512]{1,2,0:T(8,128)(2,1)}), bf16[8,128,512]{1,2,0:T(8,128)(2,1)}, u32[]{:S(2)}, u32[]{:S(2)}) async-start(bf16[8,128,512]{1,2,0:T(8,128)(2,1)} %bitcast.33), calls=%async_computation | async-start | bytes 2097152 | tf_op jit(solution)/shard_map/all_to_all | solution.py:16
  54.1 43.8 %copy-start = (bf16[128,4096]{1,0:T(8,128)(2,1)}, bf16[128,4096]{1,0:T(8,128)(2,1)S(1)}, u32[]{:S(2)}) copy-start(bf16[128,4096]{1,0:T(8,128)(2,1)S(1)} %collective-permute-done) | copy-start | bytes 3145732
  55.1 51.7 %collective-permute-start.1 = (bf16[64,4096]{1,0:T(8,128)(2,1)}, bf16[64,4096]{1,0:T(8,128)(2,1)}, u32[]{:S(2)}, u32[]{:S(2)}) collective-permute-start(bf16[64,4096]{1,0:T(8,128)(2,1)} %slice.18), channel_id=1, source_target_pairs={{0,38},{2,0},{4,2},{6,4},{32,6},{34,32},{36,34},{38,36},{1,39},{3,... | collective-permute-start | bytes 1572872 | tf_op jit(solution)/shard_map/ppermute | solution.py:12
  59.1 49.5 %collective-permute-start.3 = (bf16[64,4096]{1,0:T(8,128)(2,1)}, bf16[64,4096]{1,0:T(8,128)(2,1)}, u32[]{:S(2)}, u32[]{:S(2)}) collective-permute-start(bf16[64,4096]{1,0:T(8,128)(2,1)} %slice.19), channel_id=1, source_target_pairs={{0,2},{2,4},{4,6},{6,32},{32,34},{34,36},{36,38},{38,0},{1,3},{3,5... | collective-permute-start | bytes 1572872 | tf_op jit(solution)/shard_map/ppermute | solution.py:12
  99.6 30.1 %all-to-all-start.5 = ((bf16[4,4,32,2048]{3,2,1,0:T(8,128)(2,1)}), bf16[4,4,32,2048]{3,2,1,0:T(8,128)(2,1)S(1)}, u32[]{:S(2)}, u32[]{:S(2)}) async-start(bf16[4,4,32,2048]{3,2,1,0:T(8,128)(2,1)} %bitcast.31), calls=%async_computation.5 | async-start | bytes 4194304 | tf_op jit(solution)/shard_map/all_to_all | solution.py:16
  129.7 30.4 %all-to-all-start.2 = ((bf16[4,4,32,2048]{3,2,1,0:T(8,128)(2,1)}), bf16[4,4,32,2048]{3,2,1,0:T(8,128)(2,1)}, u32[]{:S(2)}, u32[]{:S(2)}) async-start(bf16[4,4,32,2048]{3,2,1,0:T(8,128)(2,1)} %bitcast.32), calls=%async_computation.2 | async-start | bytes 4194304 | tf_op jit(solution)/shard_map/all_to_all | solution.py:16
  160.1 17.7 %all-to-all-start.6 = ((bf16[4,32,2048]{2,1,0:T(8,128)(2,1)}), bf16[4,32,2048]{2,1,0:T(8,128)(2,1)S(1)}, u32[]{:S(2)}, u32[]{:S(2)}) async-start(bf16[4,32,2048]{2,1,0:T(8,128)(2,1)} %reduce_sum.50), calls=%async_computation.6 | async-start | bytes 1048576 | tf_op jit(solution)/shard_map/all_to_all | solution.py:16
  177.8 16.4 %all-to-all-start.3 = ((bf16[4,32,2048]{2,1,0:T(8,128)(2,1)}), bf16[4,32,2048]{2,1,0:T(8,128)(2,1)S(1)}, u32[]{:S(2)}, u32[]{:S(2)}) async-start(bf16[4,32,2048]{2,1,0:T(8,128)(2,1)} %reduce_sum.48), calls=%async_computation.3 | async-start | bytes 1048576 | tf_op jit(solution)/shard_map/all_to_all | solution.py:16
  194.2 38.2 %all-to-all-start.1 = ((bf16[4,1024,128]{1,2,0:T(8,128)(2,1)}), bf16[4,1024,128]{1,2,0:T(8,128)(2,1)S(1)}, u32[]{:S(2)}, u32[]{:S(2)}) async-start(bf16[4,1024,128]{1,2,0:T(8,128)(2,1)} %bitcast.9), calls=%async_computation.1 | async-start | bytes 2097152 | tf_op jit(solution)/shard_map/all_to_all | solution.py:16
  197.8 30.8 %collective-permute-start.5 = (bf16[32,2048]{1,0:T(8,128)(2,1)S(1)}, bf16[32,2048]{1,0:T(8,128)(2,1)S(1)}, u32[]{:S(2)}, u32[]{:S(2)}) collective-permute-start(bf16[32,2048]{1,0:T(8,128)(2,1)S(1)} %reduce_sum.51), channel_id=1, source_target_pairs={{0,32},{32,0},{1,33},{33,1},{2,34},{34,2},{3,35},{35,3},{4,36},{36... | collective-permute-start | bytes 393224 | tf_op jit(solution)/shard_map/ppermute | solution.py:12
  203.0 35.1 %collective-permute-start.4 = (bf16[32,2048]{1,0:T(8,128)(2,1)S(1)}, bf16[32,2048]{1,0:T(8,128)(2,1)S(1)}, u32[]{:S(2)}, u32[]{:S(2)}) collective-permute-start(bf16[32,2048]{1,0:T(8,128)(2,1)S(1)} %reduce_sum.49), channel_id=1, source_target_pairs={{0,32},{32,0},{1,33},{33,1},{2,34},{34,2},{3,35},{35,3},{4,36},{36... | collective-permute-start | bytes 393224 | tf_op jit(solution)/shard_map/ppermute | solution.py:12
  233.2 12.4 %all-to-all-start.7 = ((bf16[4,32,2048]{2,1,0:T(8,128)(2,1)}), bf16[4,32,2048]{2,1,0:T(8,128)(2,1)S(1)}, u32[]{:S(2)}, u32[]{:S(2)}) async-start(bf16[4,32,2048]{2,1,0:T(8,128)(2,1)} %broadcast_in_dim.5), calls=%async_computation.7 | async-start | bytes 1048576 | tf_op jit(solution)/shard_map/all_to_all | solution.py:16
  246.5 11.5 %all-to-all-start.4 = ((bf16[4,32,2048]{2,1,0:T(8,128)(2,1)}), bf16[4,32,2048]{2,1,0:T(8,128)(2,1)S(1)}, u32[]{:S(2)}, u32[]{:S(2)}) async-start(bf16[4,32,2048]{2,1,0:T(8,128)(2,1)} %broadcast_in_dim.4), calls=%async_computation.4 | async-start | bytes 1048576 | tf_op jit(solution)/shard_map/all_to_all | solution.py:16
Sparse Core Ops, SparseCore 0:
  9.9 48.8 all-gather.2
  60.6 32.7 all-gather.4
where the time goes:
time: 267 us; the launch traced here: 266 us
  waiting for transfers between devices  129 us (48%)
  starting transfers between devices  52.7 us (20%)
  local copies, waits for them, and re-layouts  36.6 us (14%)
  matrix products  20.5 us (8%)
  between operations  14.1 us (5%)
  other arithmetic  13.3 us (5%)
    all_to_all x8, waiting for transfers between devices, exchange(): return lax.all_to_all(v, axis, split_axis=0, concat_axis=0, tiled=True)  74.8 us
    all_to_all x8, starting transfers between devices, exchange(): return lax.all_to_all(v, axis, split_axis=0, concat_axis=0, tiled=True)  37.4 us
    all_gather x2, waiting for transfers between devices, local(): lax.all_gather(g[:, lo:hi], ('y', 'c'), axis=0, tiled=True)  28.4 us
    ppermute x6, waiting for transfers between devices, shift(): return lax.ppermute(v, axis, [(i, (i + by) % n) for i in range(n)])  24.7 us
    unnamed x14, local copies, waits for them, and re-layouts  18.8 us
    ppermute x6, starting transfers between devices, shift(): return lax.ppermute(v, axis, [(i, (i + by) % n) for i in range(n)])  15.3 us
    dot_general x2, matrix products, local(): lax.dot_general(acts, gj, (((0,), (0,)), ((), ())), preferred_element_typ...  10.5 us
    dot_general x1, matrix products, local(): lax.dot_general(gall, w, (((1,), (1,)), ((), ())), preferred_element_type...  10.1 us
  transfers between devices with their start and end apart: 16, of which 10 were waited for; matrix products, arithmetic and copies ran while one was open for 25% of the time, Pallas kernels for 0%

commit v1 on v0

--- a/solution.py
+++ b/solution.py
@@ -42,7 +42,13 @@
         size = size * feats // sum(CHUNKS)
         cuts.append((at, at + size))
         at += size
-    g_cols = [lax.all_gather(g[:, lo:hi], ("y", "c"), axis=0, tiled=True) for lo, hi in cuts]
+    g_cols = [
+        jnp.concatenate(
+            lax.all_to_all(jnp.stack([g[:, lo:hi]] * lax.axis_size(("y", "c"))), ("y", "c"), 0, 0),
+            axis=0,
+        )
+        for lo, hi in cuts
+    ]
     a = a.reshape(toks, 4, 4, 2, heads).transpose(1, 3, 0, 2, 4).reshape(8, toks, 4 * heads)
     acts = exchange(a, ("y", "c")).reshape(8 * toks, 4 * heads)
     w_parts = around(w_out, RING8)

time: 267 us -> 302 us (1.13)
  blocking collectives: 0 us -> 53.6 us
  waiting for transfers between devices: 129 us -> 114 us
  between operations: 14.1 us -> 0.73 us
  starting transfers between devices: 52.7 us -> 58.9 us
    all_to_all x0 -> x1, blocking collectives: none -> 53.6 us  [local(): lax.all_to_all(jnp.stack([g[:, lo:hi]] * lax.axis_size(('y', 'c'))), ('y'...]
    all_gather x2 -> x0, waiting for transfers between devices: 28.4 us -> none  [local(): lax.all_gather(g[:, lo:hi], ('y', 'c'), axis=0, tiled=True)]
    ppermute x6, waiting for transfers between devices: 24.7 us -> 43.3 us  [shift(): return lax.ppermute(v, axis, [(i, (i + by) % n) for i in range(n)])]
    all_to_all x8, waiting for transfers between devices: 74.8 us -> 62.1 us  [exchange(): return lax.all_to_all(v, axis, split_axis=0, concat_axis=0, tiled=True)]
    all_to_all x0 -> x1, waiting for transfers between devices: none -> 9.17 us  [local(): lax.all_to_all(jnp.stack([g[:, lo:hi]] * lax.axis_size(('y', 'c'))), ('y'...]
    another operation x0 -> x4, local copies, waits for them, and re-layouts: none -> 6.95 us  [the longest x2 3.88 us: local(): a.reshape(toks, 4, 4, 2, heads).transpose(1, 3, 0, 2, 4)]
    all_to_all x0 -> x1, starting transfers between devices: none -> 4.55 us  [local(): lax.all_to_all(jnp.stack([g[:, lo:hi]] * lax.axis_size(('y', 'c'))), ('y'...]
    unnamed x14 -> x17, local copies, waits for them, and re-layouts: 18.8 us -> 16.6 us
  transfers between devices with their start and end apart: 16 -> 15, of which waited for: 10 -> 11; matrix products, arithmetic and copies ran while one was open for 25% -> 21% of each run, Pallas kernels for 0% -> 0%
where the time goes in v1:
time: 302 us; the launch traced here: 301 us
  waiting for transfers between devices  114 us (38%)
  starting transfers between devices  58.9 us (20%)
  blocking collectives  53.6 us (18%)
  local copies, waits for them, and re-layouts  38.7 us (13%)
  matrix products  20.8 us (7%)
  other arithmetic  13.3 us (4%)
    all_to_all x8, waiting for transfers between devices, exchange(): return lax.all_to_all(v, axis, split_axis=0, concat_axis=0, tiled=True)  62.1 us
    all_to_all x1, blocking collectives, local(): lax.all_to_all(jnp.stack([g[:, lo:hi]] * lax.axis_size(('y', 'c'))), ('y'...  53.6 us
    ppermute x6, waiting for transfers between devices, shift(): return lax.ppermute(v, axis, [(i, (i + by) % n) for i in range(n)])  43.3 us
    all_to_all x8, starting transfers between devices, exchange(): return lax.all_to_all(v, axis, split_axis=0, concat_axis=0, tiled=True)  38.6 us
    unnamed x17, local copies, waits for them, and re-layouts  16.6 us
    ppermute x6, starting transfers between devices, shift(): return lax.ppermute(v, axis, [(i, (i + by) % n) for i in range(n)])  15.7 us
    dot_general x2, matrix products, local(): lax.dot_general(acts, gj, (((0,), (0,)), ((), ())), preferred_element_typ...  10.8 us
    dot_general x1, matrix products, local(): lax.dot_general(gall, w, (((1,), (1,)), ((), ())), preferred_element_type...  10.1 us
  transfers between devices with their start and end apart: 15, of which 11 were waited for; matrix products, arithmetic and copies ran while one was open for 21% of the time, Pallas kernels for 0%

profile of v1, /device:TPU:2, one launch (start us, length us, event | category | flops | bytes accessed | tf_op | source)
XLA Modules:
  0.0 300.6 jit_solution(6989669576942418693)
XLA Ops:
  4.5 4.5 %all-to-all-start.2 = ((bf16[8,128,512]{1,2,0:T(8,128)(2,1)}), bf16[8,128,512]{1,2,0:T(8,128)(2,1)S(1)}, u32[]{:S(2)}, u32[]{:S(2)}) async-start(bf16[8,128,512]{1,2,0:T(8,128)(2,1)} %bitcast.4), calls=%async_computation.2 | async-start | bytes 2097152 | tf_op jit(solution)/shard_map/all_to_all | solution.py:16
  10.3 14.7 %all-to-all-done.2 = bf16[8,128,512]{1,2,0:T(8,128)(2,1)S(1)} async-done(((bf16[8,128,512]{1,2,0:T(8,128)(2,1)}), bf16[8,128,512]{1,2,0:T(8,128)(2,1)S(1)}, u32[]{:S(2)}, u32[]{:S(2)}) %all-to-all-start.2) | async-done | bytes 1048608 | tf_op jit(solution)/shard_map/all_to_all | solution.py:16
  25.5 53.6 %all_to_all.50 = bf16[8,128,2048]{2,1,0:T(8,128)(2,1)} all-to-all(bf16[8,128,2048]{2,1,0:T(8,128)(2,1)S(1)} %stack.4), channel_id=1, replica_groups=mesh['x'=4,'h'=2,'y'=4,'l'=4,'c'=2] {'y','c'}, dimensions={0} | all-to-all | bytes 8388608 | tf_op jit(solution)/shard_map/all_to_all | solution.py:47
  81.6 4.5 %all-to-all-start.1 = ((bf16[8,128,2048]{2,1,0:T(8,128)(2,1)}), bf16[8,128,2048]{2,1,0:T(8,128)(2,1)}, u32[]{:S(2)}, u32[]{:S(2)}) async-start(bf16[8,128,2048]{2,1,0:T(8,128)(2,1)} %stack.5), calls=%async_computation.1 | async-start | bytes 8388608 | tf_op jit(solution)/shard_map/all_to_all | solution.py:47
  86.2 5.9 %collective-permute-start = (bf16[128,4096]{1,0:T(8,128)(2,1)S(1)}, bf16[128,4096]{1,0:T(8,128)(2,1)S(1)}, u32[]{:S(2)}, u32[]{:S(2)}) collective-permute-start(bf16[128,4096]{1,0:T(8,128)(2,1)S(1)} %copy-done.1), channel_id=1, source_target_pairs={{0,38},{2,0},{4,2},{6,4},{32,6},{34,32},{36,34},{38,36},{1,39},{3,... | collective-permute-start | bytes 3145736 | tf_op jit(solution)/shard_map/ppermute | solution.py:12
  95.5 19.5 %collective-permute-done = bf16[128,4096]{1,0:T(8,128)(2,1)S(1)} collective-permute-done((bf16[128,4096]{1,0:T(8,128)(2,1)S(1)}, bf16[128,4096]{1,0:T(8,128)(2,1)S(1)}, u32[]{:S(2)}, u32[]{:S(2)}) %collective-permute-start) | collective-permute-done | bytes 1048608 | tf_op jit(solution)/shard_map/ppermute | solution.py:12
  120.5 6.2 %bitcast_convert_fusion = bf16[512,2048]{1,0:T(8,128)(2,1)} fusion(bf16[8,128,512]{1,2,0:T(8,128)(2,1)} %copy-done.2, bf16[8,128,2048]{2,1,0:T(8,128)(2,1)} %all_to_all.50), kind=kOutput, calls=%fused_computation.1 | convolution fusion | flops 2148532224 | bytes 7340032 | tf_op jit(solution)/shard_map/dot_general | solution.py:59
  126.7 9.2 %all-to-all-done.1 = bf16[8,128,2048]{2,1,0:T(8,128)(2,1)} async-done(((bf16[8,128,2048]{2,1,0:T(8,128)(2,1)}), bf16[8,128,2048]{2,1,0:T(8,128)(2,1)}, u32[]{:S(2)}, u32[]{:S(2)}) %all-to-all-start.1) | async-done | bytes 4194336 | tf_op jit(solution)/shard_map/all_to_all | solution.py:47
  135.9 4.6 %convolution_convert_fusion = bf16[2048,512]{0,1:T(8,128)(2,1)S(1)} fusion(bf16[1024,2048]{1,0:T(8,128)(2,1)} %bitcast.2, bf16[1024,512]{1,0:T(8,128)(2,1)S(1)} %bitcast.42), kind=kOutput, calls=%fused_computation.4 | convolution fusion | flops 2148532224 | bytes 7340032 | tf_op jit(solution)/shard_map/dot_general | solution.py:59
  142.1 4.9 %all-to-all-start.7 = ((bf16[4,4,32,2048]{3,2,1,0:T(8,128)(2,1)}), bf16[4,4,32,2048]{3,2,1,0:T(8,128)(2,1)S(1)}, u32[]{:S(2)}, u32[]{:S(2)}) async-start(bf16[4,4,32,2048]{3,2,1,0:T(8,128)(2,1)} %bitcast.35), calls=%async_computation.7 | async-start | bytes 4194304 | tf_op jit(solution)/shard_map/all_to_all | solution.py:16
  157.3 14.6 %all-to-all-done.7 = bf16[4,4,32,2048]{3,2,1,0:T(8,128)(2,1)S(1)} async-done(((bf16[4,4,32,2048]{3,2,1,0:T(8,128)(2,1)}), bf16[4,4,32,2048]{3,2,1,0:T(8,128)(2,1)S(1)}, u32[]{:S(2)}, u32[]{:S(2)}) %all-to-all-start.7) | async-done | bytes 2097184 | tf_op jit(solution)/shard_map/all_to_all | solution.py:16
  171.9 5.9 %all-to-all-start.4 = ((bf16[4,4,32,2048]{3,2,1,0:T(8,128)(2,1)}), bf16[4,4,32,2048]{3,2,1,0:T(8,128)(2,1)}, u32[]{:S(2)}, u32[]{:S(2)}) async-start(bf16[4,4,32,2048]{3,2,1,0:T(8,128)(2,1)} %bitcast.36), calls=%async_computation.4 | async-start | bytes 4194304 | tf_op jit(solution)/shard_map/all_to_all | solution.py:16
  187.5 14.5 %all-to-all-done.4 = bf16[4,4,32,2048]{3,2,1,0:T(8,128)(2,1)} async-done(((bf16[4,4,32,2048]{3,2,1,0:T(8,128)(2,1)}), bf16[4,4,32,2048]{3,2,1,0:T(8,128)(2,1)}, u32[]{:S(2)}, u32[]{:S(2)}) %all-to-all-start.4) | async-done | bytes 2097184 | tf_op jit(solution)/shard_map/all_to_all | solution.py:16
  202.0 5.3 %all-to-all-start.8 = ((bf16[4,32,2048]{2,1,0:T(8,128)(2,1)}), bf16[4,32,2048]{2,1,0:T(8,128)(2,1)S(1)}, u32[]{:S(2)}, u32[]{:S(2)}) async-start(bf16[4,32,2048]{2,1,0:T(8,128)(2,1)} %reduce_sum.50), calls=%async_computation.8 | async-start | bytes 1048576 | tf_op jit(solution)/shard_map/all_to_all | solution.py:16
  208.4 7.8 %pad_maximum_fusion = bf16[1024,4096]{1,0:T(8,128)(2,1)} fusion(bf16[1024,2048]{1,0:T(8,128)(2,1)} %bitcast.2, bf16[1024,2048]{1,0:T(8,128)(2,1)} %bitcast.34), kind=kLoop, calls=%fused_computation | loop fusion | flops 16777216 | bytes 16777216 | tf_op jit(solution)/shard_map/concatenate | solution.py:70
  219.4 4.8 %all-to-all-start.5 = ((bf16[4,32,2048]{2,1,0:T(8,128)(2,1)}), bf16[4,32,2048]{2,1,0:T(8,128)(2,1)S(1)}, u32[]{:S(2)}, u32[]{:S(2)}) async-start(bf16[4,32,2048]{2,1,0:T(8,128)(2,1)} %reduce_sum.48), calls=%async_computation.5 | async-start | bytes 1048576 | tf_op jit(solution)/shard_map/all_to_all | solution.py:16
  224.2 10.1 %fusion.2 = bf16[1024,512]{0,1:T(8,128)(2,1)} fusion(bf16[1024,4096]{1,0:T(8,128)(2,1)} %pad_maximum_fusion, bf16[1024,4096]{1,0:T(8,128)(2,1)} %constant_dynamic-update-slice_fusion, s32[]{:T(128)S(6)} %select_n.3), kind=kOutput, calls=%fused_computation.7 | convolution fusion | flops 4295491584 | bytes 13631492 | tf_op jit(solution)/shard_map/dot_general | solution.py:71
  239.4 5.1 %collective-permute-start.5 = (bf16[32,2048]{1,0:T(8,128)(2,1)S(1)}, bf16[32,2048]{1,0:T(8,128)(2,1)S(1)}, u32[]{:S(2)}, u32[]{:S(2)}) collective-permute-start(bf16[32,2048]{1,0:T(8,128)(2,1)S(1)} %reduce_sum.51), channel_id=1, source_target_pairs={{0,32},{32,0},{1,33},{33,1},{2,34},{34,2},{3,35},{35,3},{4,36},{36... | collective-permute-start | bytes 393224 | tf_op jit(solution)/shard_map/ppermute | solution.py:12
  245.6 23.7 %collective-permute-done.5 = bf16[32,2048]{1,0:T(8,128)(2,1)S(1)} collective-permute-done((bf16[32,2048]{1,0:T(8,128)(2,1)S(1)}, bf16[32,2048]{1,0:T(8,128)(2,1)S(1)}, u32[]{:S(2)}, u32[]{:S(2)}) %collective-permute-start.5) | collective-permute-done | bytes 131104 | tf_op jit(solution)/shard_map/ppermute | solution.py:12
  269.4 4.5 %all-to-all-done.3 = bf16[4,1024,128]{1,2,0:T(8,128)(2,1)S(1)} async-done(((bf16[4,1024,128]{1,2,0:T(8,128)(2,1)}), bf16[4,1024,128]{1,2,0:T(8,128)(2,1)S(1)}, u32[]{:S(2)}, u32[]{:S(2)}) %all-to-all-start.3) | async-done | bytes 1048608 | tf_op jit(solution)/shard_map/all_to_all | solution.py:16
  274.8 4.9 %all-to-all-start.9 = ((bf16[4,32,2048]{2,1,0:T(8,128)(2,1)}), bf16[4,32,2048]{2,1,0:T(8,128)(2,1)S(1)}, u32[]{:S(2)}, u32[]{:S(2)}) async-start(bf16[4,32,2048]{2,1,0:T(8,128)(2,1)} %broadcast_in_dim.5), calls=%async_computation.9 | async-start | bytes 1048576 | tf_op jit(solution)/shard_map/all_to_all | solution.py:16
  279.7 7.5 %all-to-all-done.9 = bf16[4,32,2048]{2,1,0:T(8,128)(2,1)S(1)} async-done(((bf16[4,32,2048]{2,1,0:T(8,128)(2,1)}), bf16[4,32,2048]{2,1,0:T(8,128)(2,1)S(1)}, u32[]{:S(2)}, u32[]{:S(2)}) %all-to-all-start.9) | async-done | bytes 524320 | tf_op jit(solution)/shard_map/all_to_all | solution.py:16
  288.0 4.9 %all-to-all-start.6 = ((bf16[4,32,2048]{2,1,0:T(8,128)(2,1)}), bf16[4,32,2048]{2,1,0:T(8,128)(2,1)S(1)}, u32[]{:S(2)}, u32[]{:S(2)}) async-start(bf16[4,32,2048]{2,1,0:T(8,128)(2,1)} %broadcast_in_dim.4), calls=%async_computation.6 | async-start | bytes 1048576 | tf_op jit(solution)/shard_map/all_to_all | solution.py:16
  295.2 4.4 %all-to-all-done.6 = bf16[4,32,2048]{2,1,0:T(8,128)(2,1)S(1)} async-done(((bf16[4,32,2048]{2,1,0:T(8,128)(2,1)}), bf16[4,32,2048]{2,1,0:T(8,128)(2,1)S(1)}, u32[]{:S(2)}, u32[]{:S(2)}) %all-to-all-start.6) | async-done | bytes 524320 | tf_op jit(solution)/shard_map/all_to_all | solution.py:16
  (50 shorter events, 54.4 us)
Async XLA Ops:
  4.5 20.4 %all-to-all-start.2 = ((bf16[8,128,512]{1,2,0:T(8,128)(2,1)}), bf16[8,128,512]{1,2,0:T(8,128)(2,1)S(1)}, u32[]{:S(2)}, u32[]{:S(2)}) async-start(bf16[8,128,512]{1,2,0:T(8,128)(2,1)} %bitcast.4), calls=%async_computation.2 | async-start | bytes 2097152 | tf_op jit(solution)/shard_map/all_to_all | solution.py:16
  25.0 56.7 %copy-start.2 = (bf16[8,128,512]{1,2,0:T(8,128)(2,1)}, bf16[8,128,512]{1,2,0:T(8,128)(2,1)S(1)}, u32[]{:S(2)}) copy-start(bf16[8,128,512]{1,2,0:T(8,128)(2,1)S(1)} %all-to-all-done.2) | copy-start | bytes 3145732
  79.1 7.1 %copy-start.1 = (bf16[128,4096]{1,0:T(8,128)(2,1)S(1)}, bf16[128,4096]{1,0:T(8,128)(2,1)}, u32[]{:S(2)}) copy-start(bf16[128,4096]{1,0:T(8,128)(2,1)} %param.5) | copy-start | bytes 3145732
  81.6 54.2 %all-to-all-start.1 = ((bf16[8,128,2048]{2,1,0:T(8,128)(2,1)}), bf16[8,128,2048]{2,1,0:T(8,128)(2,1)}, u32[]{:S(2)}, u32[]{:S(2)}) async-start(bf16[8,128,2048]{2,1,0:T(8,128)(2,1)} %stack.5), calls=%async_computation.1 | async-start | bytes 8388608 | tf_op jit(solution)/shard_map/all_to_all | solution.py:47
  86.2 28.8 %collective-permute-start = (bf16[128,4096]{1,0:T(8,128)(2,1)S(1)}, bf16[128,4096]{1,0:T(8,128)(2,1)S(1)}, u32[]{:S(2)}, u32[]{:S(2)}) collective-permute-start(bf16[128,4096]{1,0:T(8,128)(2,1)S(1)} %copy-done.1), channel_id=1, source_target_pairs={{0,38},{2,0},{4,2},{6,4},{32,6},{34,32},{36,34},{38,36},{1,39},{3,... | collective-permute-start | bytes 3145736 | tf_op jit(solution)/shard_map/ppermute | solution.py:12
  92.1 27.5 %collective-permute-start.2 = (bf16[128,4096]{1,0:T(8,128)(2,1)S(1)}, bf16[128,4096]{1,0:T(8,128)(2,1)S(1)}, u32[]{:S(2)}, u32[]{:S(2)}) collective-permute-start(bf16[128,4096]{1,0:T(8,128)(2,1)S(1)} %copy-done.1), channel_id=1, source_target_pairs={{0,2},{2,4},{4,6},{6,32},{32,34},{34,36},{36,38},{38,0},{1,3},{3,5... | collective-permute-start | bytes 3145736 | tf_op jit(solution)/shard_map/ppermute | solution.py:12
  115.0 25.4 %copy-start = (bf16[128,4096]{1,0:T(8,128)(2,1)}, bf16[128,4096]{1,0:T(8,128)(2,1)S(1)}, u32[]{:S(2)}) copy-start(bf16[128,4096]{1,0:T(8,128)(2,1)S(1)} %collective-permute-done) | copy-start | bytes 3145732
  115.9 33.3 %collective-permute-start.1 = (bf16[64,4096]{1,0:T(8,128)(2,1)}, bf16[64,4096]{1,0:T(8,128)(2,1)}, u32[]{:S(2)}, u32[]{:S(2)}) collective-permute-start(bf16[64,4096]{1,0:T(8,128)(2,1)} %slice.18), channel_id=1, source_target_pairs={{0,38},{2,0},{4,2},{6,4},{32,6},{34,32},{36,34},{38,36},{1,39},{3,... | collective-permute-start | bytes 1572872 | tf_op jit(solution)/shard_map/ppermute | solution.py:12
  119.6 16.2 %copy-start.3 = (bf16[8,128,512]{2,1,0:T(8,128)(2,1)S(1)}, bf16[8,128,512]{2,1,0:T(8,128)(2,1)}, u32[]{:S(2)}) copy-start(bf16[8,128,512]{2,1,0:T(8,128)(2,1)} %copy.16) | copy-start | bytes 3145732
  120.5 30.7 %collective-permute-start.3 = (bf16[64,4096]{1,0:T(8,128)(2,1)}, bf16[64,4096]{1,0:T(8,128)(2,1)}, u32[]{:S(2)}, u32[]{:S(2)}) collective-permute-start(bf16[64,4096]{1,0:T(8,128)(2,1)} %slice.19), channel_id=1, source_target_pairs={{0,2},{2,4},{4,6},{6,32},{32,34},{34,36},{36,38},{38,0},{1,3},{3,5... | collective-permute-start | bytes 1572872 | tf_op jit(solution)/shard_map/ppermute | solution.py:12
  142.1 29.8 %all-to-all-start.7 = ((bf16[4,4,32,2048]{3,2,1,0:T(8,128)(2,1)}), bf16[4,4,32,2048]{3,2,1,0:T(8,128)(2,1)S(1)}, u32[]{:S(2)}, u32[]{:S(2)}) async-start(bf16[4,4,32,2048]{3,2,1,0:T(8,128)(2,1)} %bitcast.35), calls=%async_computation.7 | async-start | bytes 4194304 | tf_op jit(solution)/shard_map/all_to_all | solution.py:16
  171.9 30.1 %all-to-all-start.4 = ((bf16[4,4,32,2048]{3,2,1,0:T(8,128)(2,1)}), bf16[4,4,32,2048]{3,2,1,0:T(8,128)(2,1)}, u32[]{:S(2)}, u32[]{:S(2)}) async-start(bf16[4,4,32,2048]{3,2,1,0:T(8,128)(2,1)} %bitcast.36), calls=%async_computation.4 | async-start | bytes 4194304 | tf_op jit(solution)/shard_map/all_to_all | solution.py:16
  202.0 17.4 %all-to-all-start.8 = ((bf16[4,32,2048]{2,1,0:T(8,128)(2,1)}), bf16[4,32,2048]{2,1,0:T(8,128)(2,1)S(1)}, u32[]{:S(2)}, u32[]{:S(2)}) async-start(bf16[4,32,2048]{2,1,0:T(8,128)(2,1)} %reduce_sum.50), calls=%async_computation.8 | async-start | bytes 1048576 | tf_op jit(solution)/shard_map/all_to_all | solution.py:16
  219.4 16.4 %all-to-all-start.5 = ((bf16[4,32,2048]{2,1,0:T(8,128)(2,1)}), bf16[4,32,2048]{2,1,0:T(8,128)(2,1)S(1)}, u32[]{:S(2)}, u32[]{:S(2)}) async-start(bf16[4,32,2048]{2,1,0:T(8,128)(2,1)} %reduce_sum.48), calls=%async_computation.5 | async-start | bytes 1048576 | tf_op jit(solution)/shard_map/all_to_all | solution.py:16
  235.8 38.1 %all-to-all-start.3 = ((bf16[4,1024,128]{1,2,0:T(8,128)(2,1)}), bf16[4,1024,128]{1,2,0:T(8,128)(2,1)S(1)}, u32[]{:S(2)}, u32[]{:S(2)}) async-start(bf16[4,1024,128]{1,2,0:T(8,128)(2,1)} %bitcast.11), calls=%async_computation.3 | async-start | bytes 2097152 | tf_op jit(solution)/shard_map/all_to_all | solution.py:16
  239.4 29.9 %collective-permute-start.5 = (bf16[32,2048]{1,0:T(8,128)(2,1)S(1)}, bf16[32,2048]{1,0:T(8,128)(2,1)S(1)}, u32[]{:S(2)}, u32[]{:S(2)}) collective-permute-start(bf16[32,2048]{1,0:T(8,128)(2,1)S(1)} %reduce_sum.51), channel_id=1, source_target_pairs={{0,32},{32,0},{1,33},{33,1},{2,34},{34,2},{3,35},{35,3},{4,36},{36... | collective-permute-start | bytes 393224 | tf_op jit(solution)/shard_map/ppermute | solution.py:12
  244.6 35.1 %collective-permute-start.4 = (bf16[32,2048]{1,0:T(8,128)(2,1)S(1)}, bf16[32,2048]{1,0:T(8,128)(2,1)S(1)}, u32[]{:S(2)}, u32[]{:S(2)}) collective-permute-start(bf16[32,2048]{1,0:T(8,128)(2,1)S(1)} %reduce_sum.49), channel_id=1, source_target_pairs={{0,32},{32,0},{1,33},{33,1},{2,34},{34,2},{3,35},{35,3},{4,36},{36... | collective-permute-start | bytes 393224 | tf_op jit(solution)/shard_map/ppermute | solution.py:12
  274.8 12.4 %all-to-all-start.9 = ((bf16[4,32,2048]{2,1,0:T(8,128)(2,1)}), bf16[4,32,2048]{2,1,0:T(8,128)(2,1)S(1)}, u32[]{:S(2)}, u32[]{:S(2)}) async-start(bf16[4,32,2048]{2,1,0:T(8,128)(2,1)} %broadcast_in_dim.5), calls=%async_computation.9 | async-start | bytes 1048576 | tf_op jit(solution)/shard_map/all_to_all | solution.py:16
  288.0 11.5 %all-to-all-start.6 = ((bf16[4,32,2048]{2,1,0:T(8,128)(2,1)}), bf16[4,32,2048]{2,1,0:T(8,128)(2,1)S(1)}, u32[]{:S(2)}, u32[]{:S(2)}) async-start(bf16[4,32,2048]{2,1,0:T(8,128)(2,1)} %broadcast_in_dim.4), calls=%async_computation.6 | async-start | bytes 1048576 | tf_op jit(solution)/shard_map/all_to_all | solution.py:16
